TPU v7x, 256 devices: a whole 4x4x8 slice. The times are simulated.
256 devices in a mesh: ctx: 64 (over x, y_hi, z), ch: 4 (over y_lo, core).
Axes of the slice: x: 4, y: 4 (y_hi: 2, y_lo: 2; y = y_hi * 2 + y_lo), z: 8, core: 2. Of those that a mesh axis runs over, the one named last changes fastest.
Arguments:
- inputs: bfloat16 [32, 16, 8192], P(None, 'ch', 'ctx'), may hold values from -0.0390625 to 0.0390625
- short_filter: float32 [3, 32, 16], P(None, None, 'ch'), may hold values from -3.5 to 3.5
- long_filter: bfloat16 [32, 8192], P(None, 'ctx'), may hold values from -0.15625 to 0.15625
- grad_out: bfloat16 [32, 16, 8192], P(None, 'ch', 'ctx'), may hold values from -6 to 6
Outputs:
- grad_in: bfloat16 [32, 16, 8192], P(None, 'ch', 'ctx')
- grad_long: float32 [32, 8192], P(None, 'ctx')
- grad_short: float32 [3, 32, 16], P(None, None, 'ch')
All inputs are finite; a program needn't handle non-finite values.
Results may differ from a plain program's by a relative error of at most 0.0031.
Values may be sent and summed in bfloat16 or wider, within the bound.
A program may use at most 128 MiB of HBM per device.

v0:
```python
import math
import jax
import jax.numpy as jnp
from jax import lax
from jax.sharding import PartitionSpec as P


def shifted(array, axis, by):
    count = lax.axis_size(axis)
    pairs = [(i, i + by) for i in range(count) if 0 <= i + by < count]
    return lax.ppermute(array, axis, pairs)


def lower_band(matrix, block_len):
    leading = matrix.shape[:-2]
    flattened = matrix.reshape(leading + (2 * block_len * block_len,))
    flattened = jnp.pad(flattened, [(0, 0)] * len(leading) + [(0, block_len)])
    skewed = flattened.reshape(leading + (block_len, 2 * block_len + 1))
    return jnp.sum(skewed[..., :block_len], axis=-2)


def shift_matrix(piece, block_len):
    leading = piece.shape[:-1]
    padded = jnp.pad(piece, [(0, 0)] * len(leading) + [(block_len, block_len + 1)])
    tiled = jnp.broadcast_to(padded[..., None, :], leading + (block_len, 3 * block_len + 1))
    flattened = tiled.reshape(leading + (block_len * (3 * block_len + 1),))[
        ..., : 3 * block_len * block_len
    ]
    skewed = flattened.reshape(leading + (block_len, 3 * block_len))
    return skewed[..., block_len:]


def per_device(inputs, short_filter, long_filter, grad_out):
    tap_count = short_filter.shape[0]
    filter_count, chan_count, shard_len = inputs.shape
    ctx_count = lax.axis_size("ctx")
    my_index = lax.axis_index("ctx")
    total_len = shard_len * ctx_count
    block_len = math.gcd(shard_len, 128)
    own_count = shard_len // block_len
    block_count = total_len // block_len
    margin = tap_count - 1
    edge = shifted(inputs[:, :, shard_len - margin :], "ctx", 1)
    extended = jnp.concatenate([edge, inputs], axis=2).astype(jnp.float32)

    def delayed(offset):
        return lax.slice_in_dim(extended, margin - offset, margin - offset + shard_len, axis=2)

    hidden = sum(
        (short_filter[offset][:, :, None] * delayed(offset) for offset in range(tap_count))
    )
    hidden = hidden.astype(jnp.bfloat16)
    grad_all, filter_all = (
        lax.all_gather(grad_out, "ctx", axis=2, tiled=True),
        lax.all_gather(long_filter, "ctx", axis=1, tiled=True),
    )
    grad_padded = jnp.pad(grad_all, ((0, 0), (0, 0), (0, total_len + block_len)))
    grad_blocks = grad_padded.reshape(filter_count, chan_count, 2 * block_count + 1, block_len)
    filter_blocks = filter_all.reshape(filter_count, block_count, block_len)

    def windows_at(first, count):
        sliced = lax.dynamic_slice_in_dim(grad_blocks, first, count + 1, axis=2)
        return jnp.concatenate([sliced[:, :, :-1], sliced[:, :, 1:]], axis=3)

    block_num = 0
    window = windows_at(my_index * own_count + block_num, block_count)
    banded = jnp.einsum("fkr,fgkj->fgrj", filter_blocks, window, preferred_element_type=jnp.float32)
    pieces = lower_band(banded, block_len)
    following = shifted(pieces[:, :, :margin], "ctx", -1)
    extended_grad = jnp.concatenate([pieces, following], axis=2)
    grad_in = sum(
        (
            short_filter[offset][:, :, None]
            * lax.slice_in_dim(extended_grad, offset, offset + shard_len, axis=2)
            for offset in range(tap_count)
        )
    )
    grad_in = grad_in.astype(jnp.bfloat16)
    local_short = jnp.stack(
        [jnp.sum(pieces * delayed(offset), axis=2) for offset in range(tap_count)]
    )
    grad_short = lax.psum(local_short, "ctx")
    hidden_shards = hidden.reshape(filter_count, chan_count, own_count, block_len)
    count = shard_len * lax.axis_size("ctx")
    first = jnp.int32(0) // block_len
    count_blocks = count // block_len
    block_num = 0
    window = windows_at(my_index * own_count + block_num, count_blocks)
    toeplitz = shift_matrix(hidden_shards[:, :, block_num], block_len)
    term = jnp.einsum("fgkj,fgrj->fkr", window, toeplitz, preferred_element_type=jnp.float32)
    own_lags = lax.psum_scatter(
        term.reshape(filter_count, count).T, "ctx", scatter_dimension=0, tiled=True
    ).T
    grad_long = lax.psum(own_lags, "ch")
    return (grad_in, grad_long, grad_short)


def solution(mesh):
    in_specs = (P(None, "ch", "ctx"), P(None, None, "ch"), P(None, "ctx"), P(None, "ch", "ctx"))
    out_specs = (P(None, "ch", "ctx"), P(None, "ctx"), P(None, None, "ch"))
    return jax.shard_map(
        per_device, mesh=mesh, in_specs=in_specs, out_specs=out_specs, check_vma=False
    )
```

profile of v0, /device:TPU:1, one launch (start us, length us, event | category | flops | bytes accessed | tf_op | source)
XLA Modules:
  0.0 729.9 jit_solution(7096233392741595054)
XLA Ops:
  7.2 0.7 all-gather.2.cloned.1.call-update
  7.9 0.0 reduce-scatter.2.cloned.1.call-start
  7.9 0.8 copy.21
  8.7 0.1 slice.72
  8.8 4.4 collective-permute-start.1
  13.2 158.3 %all_gather.7 = bf16[32,8192]{1,0:T(8,128)(2,1)S(1)} all-gather(bf16[32,128]{1,0:T(8,128)(2,1)} %param.6), channel_id=1, replica_groups=mesh['ctx'=64,'ch'=4] {'ctx'}, dimensions={1}, use_global_device_ids=true | all-gather | bytes 532480 | tf_op jit(solution)/shard_map/all_gather | solution.py:55
  171.5 0.1 copy.39
  171.6 0.7 slice_bitcast_fusion.2
  172.3 4.8 pad.12
  177.1 7.3 %reshape.40 = bf16[32,4,129,128]{3,2,1,0:T(8,128)(2,1)} reshape(bf16[32,4,16512]{2,1,0:T(4,128)(2,1)} %pad.12) | data formatting | bytes 8454144 | tf_op jit(solution)/shard_map/reshape | solution.py:58
  184.5 4.8 constant_dynamic-slice_fusion
  189.3 1.3 copy-done
  190.7 7.1 convolution_bitcast_fusion
  197.8 17.5 %copy.20 = f32[32,4,128,256]{3,2,0,1:T(8,128)} copy(f32[32,4,128,256]{2,3,1,0:T(8,128)} %convolution_bitcast_fusion) | data formatting | bytes 33554432 | tf_op jit(solution)/shard_map/fkr,fgkj->fgrj/transpose | solution.py:67
  215.2 18.2 %reshape.33 = f32[32,4,32768]{2,0,1:T(8,128)} reshape(f32[32,4,128,256]{3,2,0,1:T(8,128)} %copy.20) | data formatting | bytes 33554432 | tf_op jit(solution)/shard_map/reshape | solution.py:16
  233.5 11.4 %pad.13 = f32[32,4,32896]{2,0,1:T(8,128)} pad(f32[32,4,32768]{2,0,1:T(8,128)} %reshape.33, f32[]{:T(128)} %constant.14.clone.1), padding=0_0x0_0x0_128 | pad | bytes 33619972 | tf_op jit(solution)/shard_map/jit(_pad)/pad | solution.py:17
  244.8 26.6 %reshape.34 = f32[32,4,128,257]{3,2,0,1:T(8,128)} reshape(f32[32,4,32896]{2,0,1:T(8,128)} %pad.13) | data formatting | bytes 33685504 | tf_op jit(solution)/shard_map/reshape | solution.py:18
  271.5 4.6 slice_reduce_fusion
  276.0 1.5 collective-permute-start
  277.5 0.1 maximum_convert_fusion
  277.6 3.4 collective-permute-done
  281.1 0.3 multiply_reduce_fusion.2
  281.4 6.1 broadcast_in_dim.2
  287.5 24.6 %reshape.35 = bf16[32,4,49280]{2,0,1:T(8,128)(2,1)} reshape(bf16[32,4,128,385]{3,2,0,1:T(8,128)(2,1)} %broadcast_in_dim.2) | data formatting | bytes 25231360 | tf_op jit(solution)/shard_map/reshape | solution.py:26
  312.0 4.6 slice-done
  316.6 2.7 copy.40
  319.3 4.3 fusion
  323.6 1.6 copy.45
  325.2 0.6 copy.30
  325.9 152.7 %psum.15 = f32[3,32,4]{1,2,0:T(4,128)} all-reduce(f32[3,32,4]{1,2,0:T(4,128)S(1)} %pad_maximum_fusion.4), channel_id=1, replica_groups=mesh['ctx'=64,'ch'=4] {'ctx'}, use_global_device_ids=true, to_apply=%region_6.7 | all-reduce | flops 384 | bytes 3072 | tf_op jit(solution)/shard_map/psum | solution.py:82
  478.6 182.7 %reduce-scatter.2.cloned.1.call-done = f32[128,32]{0,1:T(8,128)} async-done(((f32[8192,32]{0,1:T(8,128)}), f32[128,32]{0,1:T(8,128)}) %reduce-scatter.2.cloned.1.call-update) | async-done | bytes 16400 | tf_op jit(solution)/shard_map/reduce_scatter | solution.py:91
  661.3 61.7 %psum.14 = f32[32,128]{1,0:T(8,128)} all-reduce(f32[32,128]{1,0:T(8,128)} %bitcast.52), channel_id=1, replica_groups=mesh['ctx'=64,'ch'=4] {'ch'}, use_global_device_ids=true, to_apply=%region_2.3 | all-reduce | flops 4096 | bytes 32768 | tf_op jit(solution)/shard_map/psum | solution.py:94
  (8 shorter events, 0.1 us)
Async XLA Ops:
  7.2 165.2 %all-gather.2.cloned.1.call-start = ((), (), s32[]{:S(2)}) async-start(), calls=%async_computation.1 | async-start | bytes 2129920 | tf_op jit(solution)/shard_map/all_gather | solution.py:54
  7.9 653.4 %reduce-scatter.2.cloned.1.call-start = ((), (), s32[]{:S(2)}) async-start(), calls=%async_computation.2 | async-start | bytes 1064960 | tf_op jit(solution)/shard_map/reduce_scatter | solution.py:91
  8.8 268.7 %collective-permute-start.1 = (bf16[32,4,2]{2,0,1:T(8,128)(2,1)S(1)}, bf16[32,4,2]{2,0,1:T(8,128)(2,1)S(1)}, u32[]{:S(2)}, u32[]{:S(2)}) collective-permute-start(bf16[32,4,2]{2,0,1:T(8,128)(2,1)S(1)} %slice.72), channel_id=1, source_target_pairs={{0,4},{4,8},{8,12},{12,16},{16,20},{20,24},{24,28},{28,32},{32,36}... | collective-permute-start | bytes 1544 | tf_op jit(solution)/shard_map/ppermute | solution.py:11
  189.3 1.4 copy-start
  276.0 5.0 collective-permute-start
  312.0 4.6 slice-start
Sparse Core Ops, SparseCore 0:
  11.4 97.2 all-gather.1
  325.4 335.9 reduce-scatter.1
where the time goes:
time: 732 us; the launch traced here: 730 us
  blocking collectives  373 us (51%)
  waiting for transfers between devices  187 us (26%)
  local copies, waits for them, and re-layouts  134 us (18%)
  between operations  14.1 us (2%)
  matrix products  11.5 us (2%)
    reduce_scatter x1, waiting for transfers between devices, per_device(): lax.psum_scatter(term.reshape(filter_count, count).T, 'ctx', scatter_dime...  183 us
    all_gather x1, blocking collectives, per_device(): lax.all_gather(long_filter, 'ctx', axis=1, tiled=True)  158 us
    psum x1, blocking collectives, per_device(): grad_short = lax.psum(local_short, 'ctx')  153 us
    psum x1, blocking collectives, per_device(): grad_long = lax.psum(own_lags, 'ch')  61.7 us
    reshape x1, local copies, waits for them, and re-layouts, lower_band(): skewed = flattened.reshape(leading + (block_len, 2 * block_len + 1))  26.6 us
    reshape x1, local copies, waits for them, and re-layouts, shift_matrix(): tiled.reshape(leading + (block_len * (3 * block_len + 1),))  24.6 us
    reshape x1, local copies, waits for them, and re-layouts, lower_band(): flattened = matrix.reshape(leading + (2 * block_len * block_len,))  18.2 us
    transpose x1, local copies, waits for them, and re-layouts, per_device(): jnp.einsum('fkr,fgkj->fgrj', filter_blocks, window, preferred_element_typ...  17.5 us
  transfers between devices with their start and end apart: 4, of which 2 were waited for; matrix products, arithmetic and copies ran while one was open for 14% of the time, Pallas kernels for 0%

commit v1 on v0

--- a/solution.py
+++ b/solution.py
@@ -50,9 +50,16 @@
         (short_filter[offset][:, :, None] * delayed(offset) for offset in range(tap_count))
     )
     hidden = hidden.astype(jnp.bfloat16)
+
+    def prepare_panel(target, across):
+        lower = jax.lax.axis_size(across)
+        big = jnp.stack(lower * [target])
+        local_out = jax.lax.all_to_all(big, across, 0, 0)
+        return jnp.concatenate(local_out, 1)
+
     grad_all, filter_all = (
         lax.all_gather(grad_out, "ctx", axis=2, tiled=True),
-        lax.all_gather(long_filter, "ctx", axis=1, tiled=True),
+        prepare_panel(long_filter, "ctx"),
     )
     grad_padded = jnp.pad(grad_all, ((0, 0), (0, 0), (0, total_len + block_len)))
     grad_blocks = grad_padded.reshape(filter_count, chan_count, 2 * block_count + 1, block_len)

time: 732 us -> 659 us (0.900)
  blocking collectives: 373 us -> 220 us
  waiting for transfers between devices: 187 us -> 248 us
  starting transfers between devices: 5.9 us -> 19.6 us
    all_gather x1 -> x0, blocking collectives: 158 us -> none  [per_device(): lax.all_gather(long_filter, 'ctx', axis=1, tiled=True)]
    all_gather x1, waiting for transfers between devices: 0.01 us -> 79 us  [per_device(): lax.all_gather(grad_out, 'ctx', axis=2, tiled=True)]
    reduce_scatter x1, waiting for transfers between devices: 183 us -> 165 us  [per_device(): lax.psum_scatter(term.reshape(filter_count, count).T, 'ctx', scatter_dime...]
    all_to_all x0 -> x1, starting transfers between devices: none -> 15.1 us  [prepare_panel(): local_out = jax.lax.all_to_all(big, across, 0, 0)]
  transfers between devices with their start and end apart: 4 -> 5, of which waited for: 2 -> 3; matrix products, arithmetic and copies ran while one was open for 14% -> 17% of each run, Pallas kernels for 0% -> 0%
where the time goes in v1:
time: 659 us; the launch traced here: 656 us
  waiting for transfers between devices  248 us (38%)
  blocking collectives  220 us (33%)
  local copies, waits for them, and re-layouts  135 us (20%)
  starting transfers between devices  19.6 us (3%)
  matrix products  14.1 us (2%)
  between operations  14.1 us (2%)
    reduce_scatter x1, waiting for transfers between devices, per_device(): lax.psum_scatter(term.reshape(filter_count, count).T, 'ctx', scatter_dime...  165 us
    psum x1, blocking collectives, per_device(): grad_short = lax.psum(local_short, 'ctx')  158 us
    all_gather x1, waiting for transfers between devices, per_device(): lax.all_gather(grad_out, 'ctx', axis=2, tiled=True)  79 us
    psum x1, blocking collectives, per_device(): grad_long = lax.psum(own_lags, 'ch')  61.7 us
    reshape x1, local copies, waits for them, and re-layouts, lower_band(): skewed = flattened.reshape(leading + (block_len, 2 * block_len + 1))  26.6 us
    reshape x1, local copies, waits for them, and re-layouts, shift_matrix(): tiled.reshape(leading + (block_len * (3 * block_len + 1),))  24.6 us
    reshape x1, local copies, waits for them, and re-layouts, lower_band(): flattened = matrix.reshape(leading + (2 * block_len * block_len,))  18.2 us
    transpose x1, local copies, waits for them, and re-layouts, per_device(): jnp.einsum('fkr,fgkj->fgrj', filter_blocks, window, preferred_element_typ...  17.5 us
  transfers between devices with their start and end apart: 5, of which 3 were waited for; matrix products, arithmetic and copies ran while one was open for 17% of the time, Pallas kernels for 0%

profile of v1, /device:TPU:1, one launch (start us, length us, event | category | flops | bytes accessed | tf_op | source)
XLA Modules:
  0.0 656.5 jit_solution(527411935190206058)
XLA Ops:
  7.2 0.7 all-gather.2.cloned.1.call-update
  7.9 1.6 stack.10
  9.5 15.1 %all-to-all-start = ((bf16[64,32,128]{2,1,0:T(8,128)(2,1)}), bf16[64,32,128]{2,1,0:T(8,128)(2,1)S(1)}, u32[]{:S(2)}, u32[]{:S(2)}) async-start(bf16[64,32,128]{2,1,0:T(8,128)(2,1)} %stack.10), calls=%async_computation | async-start | bytes 1048576 | tf_op jit(solution)/shard_map/all_to_all | solution.py:57
  24.6 0.0 reduce-scatter.2.cloned.1.call-start
  24.6 0.8 copy.22
  25.4 0.1 slice.72
  25.5 2.9 collective-permute-start.1
  28.4 0.7 slice_bitcast_fusion.2
  29.1 79.0 %all-gather.2.cloned.1.call-done = bf16[32,4,8192]{2,1,0:T(4,128)(2,1)} async-done(((bf16[32,4,128]{2,1,0:T(4,128)(2,1)}), bf16[32,4,8192]{2,1,0:T(4,128)(2,1)}) %all-gather.2.cloned.1.call-update) | async-done | bytes 2097168 | tf_op jit(solution)/shard_map/all_gather | solution.py:61
  108.1 4.9 pad.12
  113.0 7.3 %reshape.42 = bf16[32,4,129,128]{3,2,1,0:T(8,128)(2,1)} reshape(bf16[32,4,16512]{2,1,0:T(4,128)(2,1)} %pad.12) | data formatting | bytes 8454144 | tf_op jit(solution)/shard_map/reshape | solution.py:65
  120.3 6.2 constant_dynamic-slice_fusion
  126.5 9.8 %convolution_bitcast_fusion = f32[32,4,128,256]{2,3,1,0:T(8,128)} fusion(bf16[32,4,64,128]{3,2,1,0:T(8,128)(2,1)} %get-tuple-element.10, bf16[32,4,64,128]{3,2,1,0:T(8,128)(2,1)S(1)} %get-tuple-element.9, bf16[64,32,128]{2,1,0:T(8,128)(2,1)S(1)} %all-to-all-done), kind=kOutput, calls=%fused_computation | convolution fusion | flops 545259520 | bytes 21495808 | tf_op jit(solution)/shard_map/fkr,fgkj->fgrj/dot_general | solution.py:74
  136.3 17.5 %copy.21 = f32[32,4,128,256]{3,2,0,1:T(8,128)} copy(f32[32,4,128,256]{2,3,1,0:T(8,128)} %convolution_bitcast_fusion) | data formatting | bytes 33554432 | tf_op jit(solution)/shard_map/fkr,fgkj->fgrj/transpose | solution.py:74
  153.8 18.2 %reshape.35 = f32[32,4,32768]{2,0,1:T(8,128)} reshape(f32[32,4,128,256]{3,2,0,1:T(8,128)} %copy.21) | data formatting | bytes 33554432 | tf_op jit(solution)/shard_map/reshape | solution.py:16
  172.0 11.4 %pad.13 = f32[32,4,32896]{2,0,1:T(8,128)} pad(f32[32,4,32768]{2,0,1:T(8,128)} %reshape.35, f32[]{:T(128)} %constant.14.clone.1), padding=0_0x0_0x0_128 | pad | bytes 33619972 | tf_op jit(solution)/shard_map/jit(_pad)/pad | solution.py:17
  183.3 26.6 %reshape.36 = f32[32,4,128,257]{3,2,0,1:T(8,128)} reshape(f32[32,4,32896]{2,0,1:T(8,128)} %pad.13) | data formatting | bytes 33685504 | tf_op jit(solution)/shard_map/reshape | solution.py:18
  210.0 4.6 slice_reduce_fusion
  214.6 1.5 collective-permute-start
  216.1 0.1 maximum_convert_fusion
  216.1 3.4 collective-permute-done
  219.6 0.3 multiply_reduce_fusion.2
  219.9 6.1 broadcast_in_dim.2
  226.0 24.6 %reshape.37 = bf16[32,4,49280]{2,0,1:T(8,128)(2,1)} reshape(bf16[32,4,128,385]{3,2,0,1:T(8,128)(2,1)} %broadcast_in_dim.2) | data formatting | bytes 25231360 | tf_op jit(solution)/shard_map/reshape | solution.py:26
  250.5 4.6 slice-done
  255.1 2.7 copy.40
  257.8 4.3 fusion
  262.1 1.6 copy.49
  263.8 0.6 copy.31
  264.4 158.1 %psum.15 = f32[3,32,4]{1,2,0:T(4,128)} all-reduce(f32[3,32,4]{1,2,0:T(4,128)S(1)} %pad_maximum_fusion.4), channel_id=1, replica_groups=mesh['ctx'=64,'ch'=4] {'ctx'}, use_global_device_ids=true, to_apply=%region_6.7 | all-reduce | flops 384 | bytes 3072 | tf_op jit(solution)/shard_map/psum | solution.py:89
  422.5 165.3 %reduce-scatter.2.cloned.1.call-done = f32[128,32]{0,1:T(8,128)} async-done(((f32[8192,32]{0,1:T(8,128)}), f32[128,32]{0,1:T(8,128)}) %reduce-scatter.2.cloned.1.call-update) | async-done | bytes 16400 | tf_op jit(solution)/shard_map/reduce_scatter | solution.py:98
  587.9 61.7 %psum.14 = f32[32,128]{1,0:T(8,128)} all-reduce(f32[32,128]{1,0:T(8,128)} %bitcast.50), channel_id=1, replica_groups=mesh['ctx'=64,'ch'=4] {'ch'}, use_global_device_ids=true, to_apply=%region_2.3 | all-reduce | flops 4096 | bytes 32768 | tf_op jit(solution)/shard_map/psum | solution.py:101
  (7 shorter events, 0.1 us)
Async XLA Ops:
  7.2 100.9 %all-gather.2.cloned.1.call-start = ((), (), s32[]{:S(2)}) async-start(), calls=%async_computation.2 | async-start | bytes 2129920 | tf_op jit(solution)/shard_map/all_gather | solution.py:61
  9.5 117.0 %all-to-all-start = ((bf16[64,32,128]{2,1,0:T(8,128)(2,1)}), bf16[64,32,128]{2,1,0:T(8,128)(2,1)S(1)}, u32[]{:S(2)}, u32[]{:S(2)}) async-start(bf16[64,32,128]{2,1,0:T(8,128)(2,1)} %stack.10), calls=%async_computation | async-start | bytes 1048576 | tf_op jit(solution)/shard_map/all_to_all | solution.py:57
  24.6 563.3 %reduce-scatter.2.cloned.1.call-start = ((), (), s32[]{:S(2)}) async-start(), calls=%async_computation.3 | async-start | bytes 1064960 | tf_op jit(solution)/shard_map/reduce_scatter | solution.py:98
  25.5 190.6 %collective-permute-start.1 = (bf16[32,4,2]{2,0,1:T(8,128)(2,1)S(1)}, bf16[32,4,2]{2,0,1:T(8,128)(2,1)S(1)}, u32[]{:S(2)}, u32[]{:S(2)}) collective-permute-start(bf16[32,4,2]{2,0,1:T(8,128)(2,1)S(1)} %slice.72), channel_id=1, source_target_pairs={{0,4},{4,8},{8,12},{12,16},{16,20},{20,24},{24,28},{28,32},{32,36}... | collective-permute-start | bytes 1544 | tf_op jit(solution)/shard_map/ppermute | solution.py:11
  214.6 5.0 collective-permute-start
  250.5 4.6 slice-start
Sparse Core Ops, SparseCore 0:
  11.4 96.6 all-gather.1
  263.9 323.9 reduce-scatter.1
